TPU v7x, 256 devices: a whole 4x4x8 slice. The times are simulated.
256 devices in a mesh: dp: 32 (over z, y), row: 2 (over core), col: 4 (over x).
Axes of the slice: x: 4, y: 4, z: 8, core: 2. Of those that a mesh axis runs over, the one named last changes fastest.
Arguments:
- x_input: bfloat16 [32, 32, 64, 640], P('dp', 'row', 'col'), may hold values from -6 to 6
- pre_act: bfloat16 [32, 32, 64, 640], P('dp', 'row', 'col'), may hold values from -6 to 6
- out_grad: bfloat16 [32, 32, 64, 640], P('dp', 'row', 'col'), may hold values from -0.15625 to 0.15625
- conv_weight: bfloat16 [3, 3, 640, 640], replicated, may hold values from -0.078125 to 0.078125
- q_prev: float32 [5760, 2, 64], replicated, may hold values from -6 to 6
Outputs:
- p_basis: float32 [640, 2, 64], P('dp')
- q_next: float32 [5760, 2, 64], P('dp')
All inputs are finite; a program needn't handle non-finite values.
Results may differ from a plain program's by a relative error of at most 0.0036.
Values may be sent and summed in bfloat16 or wider, within the bound.
A program may use at most 128 MiB of HBM per device.

v0:
```python
import jax
import jax.numpy as jnp
from jax import lax
from jax.sharding import PartitionSpec as P


def padded_2(value, sides, width):
    for axis, dim in sides:
        size, length = (lax.axis_size(axis), value.shape[dim])
        up = [(i, (i + 1) % size) for i in range(size - 1)]
        down = [(j, i) for i, j in up]
        last = lax.slice_in_dim(value, length - width, length, axis=dim)
        leading = lax.slice_in_dim(value, 0, width, axis=dim)
        before = lax.ppermute(last, axis, up)
        after = lax.ppermute(leading, axis, down)
        value = jnp.concatenate([before, value, after], axis=dim)
    return value


def silu_slope(pre_float):
    sigma = jax.nn.sigmoid(pre_float)
    return sigma * (1.0 + pre_float * (1.0 - sigma))


def contract_first(left, right, exact):
    if exact:
        return lax.dot_general(
            left,
            right,
            (((0,), (0,)), ((), ())),
            precision=lax.Precision.HIGHEST,
            preferred_element_type=jnp.float32,
        )
    return lax.dot_general(
        left, right, (((0,), (0,)), ((), ())), preferred_element_type=jnp.float32
    )


def tap_window(padded, shift_row, shift_col, height, breadth):
    return padded[
        1 + shift_row : 1 + shift_row + height, 1 + shift_col : 1 + shift_col + breadth, :
    ].reshape(height * breadth, padded.shape[2])


def column_terms(moments, q_prev):
    return jnp.stack(
        [contract_first(moments[layer], q_prev[:, layer, :], True) for layer in range(2)], axis=1
    )


def row_terms(moments, ortho_basis):
    return jnp.stack(
        [
            jnp.dot(
                moments[layer],
                ortho_basis[:, layer, :],
                precision=lax.Precision.HIGHEST,
                preferred_element_type=jnp.float32,
            )
            for layer in range(2)
        ],
        axis=1,
    )


def gram_of(power_raw):
    return jnp.einsum(
        "mqn,mqg->qng",
        power_raw,
        power_raw,
        precision=lax.Precision.HIGHEST,
        preferred_element_type=jnp.float32,
    )


def orthonormal(power_raw, gram_matrix):
    bases = []
    for layer in range(2):
        lower = jnp.linalg.cholesky(gram_matrix[layer])
        bases.append(
            lax.linalg.triangular_solve(
                lower, power_raw[:, layer, :], left_side=False, lower=True, transpose_a=True
            )
        )
    return jnp.stack(bases, axis=1)


def on_device(x_input, pre_act, out_grad, conv_weight, q_prev):
    height, breadth, channels = (x_input.shape[1], x_input.shape[2], x_input.shape[3])
    pixels = height * breadth
    input_tile = x_input.reshape(height, breadth, channels)
    grad_tile = out_grad.reshape(height, breadth, channels)
    pre_float = pre_act.reshape(pixels, channels).astype(jnp.float32)
    hidden_flat = jax.nn.silu(pre_float).astype(jnp.bfloat16)
    grad_pad = padded_2(grad_tile, (("row", 0), ("col", 1)), 1)
    back_grad = jnp.zeros((pixels, channels), jnp.float32)
    second_taps = []
    for shift_row in (-1, 0, 1):
        for shift_col in (-1, 0, 1):
            window = tap_window(grad_pad, -shift_row, -shift_col, height, breadth)
            back_grad = back_grad + lax.dot_general(
                window,
                conv_weight[shift_row + 1, shift_col + 1],
                (((1,), (1,)), ((), ())),
                preferred_element_type=jnp.float32,
            )
            second_taps.append(contract_first(hidden_flat, window, False))
    pre_grad = (back_grad * silu_slope(pre_float)).astype(jnp.bfloat16)
    first_taps = []
    deriv_pad = padded_2(pre_grad.reshape(height, breadth, channels), (("row", 0), ("col", 1)), 1)
    input_flat = input_tile.reshape(pixels, channels)
    for shift_row in (-1, 0, 1):
        for shift_col in (-1, 0, 1):
            first_taps.append(
                contract_first(
                    input_flat,
                    tap_window(deriv_pad, -shift_row, -shift_col, height, breadth),
                    False,
                )
            )
    moments = jnp.stack(
        [
            jnp.stack(first_taps).reshape(9 * channels, channels),
            jnp.stack(second_taps).reshape(9 * channels, channels),
        ]
    )
    kernel_rows = moments.shape[1]
    owner = lax.axis_index("dp")
    basis_count = channels // lax.axis_size("dp")
    factor_count = kernel_rows // lax.axis_size("dp")
    power_raw = lax.psum(column_terms(moments, q_prev), ("dp", "row", "col"))
    ortho_basis = orthonormal(power_raw, gram_of(power_raw))
    factor_full = lax.psum(row_terms(moments, ortho_basis), ("dp", "row", "col"))
    basis_out = lax.dynamic_slice_in_dim(ortho_basis, owner * basis_count, basis_count, 0)
    factor_out = lax.dynamic_slice_in_dim(factor_full, owner * factor_count, factor_count, 0)
    return (basis_out, factor_out)


def solution(mesh):
    placed = (
        P("dp", "row", "col", None),
        P("dp", "row", "col", None),
        P("dp", "row", "col", None),
        P(),
        P(),
    )
    return jax.shard_map(
        on_device,
        mesh=mesh,
        in_specs=placed,
        out_specs=(P("dp", None, None), P("dp", None, None)),
        check_vma=False,
    )
```

profile of v0, /device:TPU:6, one launch (start us, length us, event | category | flops | bytes accessed | tf_op | source)
XLA Modules:
  0.0 655.5 jit_solution(3594010810887087729)
XLA Ops:
  7.2 0.8 slice_bitcast_fusion.9
  8.0 1.3 collective-permute-start.1
  9.3 3.0 collective-permute-start
  12.3 1.2 fusion.43
  13.5 1.2 fusion.38
  14.7 1.1 pad_maximum_fusion.11
  15.8 1.3 collective-permute-start.3
  17.1 4.5 collective-permute-start.2
  21.7 1.1 pad_maximum_fusion.5
  22.8 1.6 fusion.23
  24.5 1.4 maximum_maximum_fusion
  26.0 0.5 bitcast_dynamic-update-slice_fusion.17
  26.5 0.5 bitcast_dynamic-update-slice_fusion.16
  26.9 0.5 bitcast_dynamic-update-slice_fusion.15
  27.9 0.5 bitcast_dynamic-update-slice_fusion.13
  28.5 1.1 slice-done.4
  29.6 1.1 slice-done.5
  31.7 0.5 bitcast_dynamic-update-slice_fusion.11
  32.1 0.5 bitcast_dynamic-update-slice_fusion.10
  32.6 0.5 bitcast_dynamic-update-slice_fusion.9
  33.6 0.5 convolution_add_fusion.5
  34.5 0.5 convolution_add_fusion.3
  35.9 0.5 fusion.8
  36.4 1.4 collective-permute-start.5
  37.8 3.2 collective-permute-start.4
  41.1 8.8 %fusion.12 = f32[640,1,64]{0,2,1:T(8,128)S(1)} fusion(f32[5760,640]{1,0:T(8,128)S(1)} %bitcast.253, f32[5760,2,64]{0,2,1:T(8,128)S(1)} %copy-done.5), kind=kOutput, calls=%fused_computation.38 | convolution fusion | flops 2831155200 | bytes 16384000 | tf_op jit(solution)/shard_map/dot_general | solution.py:27
  50.0 1.3 collective-permute-start.7
  51.3 4.8 collective-permute-start.6
  56.1 1.4 collective-permute-done.6
  62.3 9.2 %fusion.9 = f32[640,1,64]{0,2,1:T(8,128)S(1)} fusion(f32[5760,640]{1,0:T(8,128)S(1)} %bitcast.249, f32[5760,2,64]{0,2,1:T(8,128)S(1)} %copy-done.5), kind=kOutput, calls=%fused_computation.37 | convolution fusion | flops 2831155200 | bytes 16384000 | tf_op jit(solution)/shard_map/dot_general | solution.py:27
  71.5 0.7 pad_maximum_fusion.7
  72.3 249.7 %all-reduce.3.cloned.1.call-done = f32[640,2,64]{0,2,1:T(8,128)} async-done(((f32[640,2,64]{0,2,1:T(8,128)}), f32[640,2,64]{0,2,1:T(8,128)}) %all-reduce.3.cloned.1.call-update) | async-done | bytes 327696 | tf_op jit(solution)/shard_map/psum | solution.py:131
  322.0 1.5 fusion.62
  323.8 5.8 cholesky.44
  329.7 0.6 compare_reduce_fusion.1
  330.3 0.7 fusion.50
  331.0 4.9 custom-call.6
  335.9 5.9 cholesky.55
  341.8 0.6 compare_reduce_fusion
  342.4 0.7 fusion.51
  343.1 4.9 custom-call.7
  348.0 1.4 fusion.45
  349.4 17.3 %convolution_bitcast_fusion = f32[5760,1,64]{0,2,1:T(8,128)S(1)} fusion(f32[5760,640]{1,0:T(8,128)} %bitcast.254, f32[64,640]{1,0:T(8,128)S(1)} %fusion.45), kind=kOutput, calls=%fused_computation | convolution fusion | flops 2831155200 | bytes 16384000 | tf_op jit(solution)/shard_map/dot_general | solution.py:54
  367.1 14.2 %convolution_bitcast_fusion.1 = f32[5760,1,64]{0,2,1:T(8,128)S(1)} fusion(f32[5760,640]{1,0:T(8,128)S(1)} %bitcast.252, f32[64,640]{1,0:T(8,128)S(1)} %fusion.46), kind=kOutput, calls=%fused_computation.1 | convolution fusion | flops 2831155200 | bytes 16384000 | tf_op jit(solution)/shard_map/dot_general | solution.py:54
  381.4 1.8 pad_maximum_fusion
  383.3 0.7 copy.11
  384.0 262.8 %all-reduce.5.cloned.1.call-done = f32[5760,2,64]{0,2,1:T(8,128)} async-done(((f32[5760,2,64]{0,2,1:T(8,128)}), f32[5760,2,64]{0,2,1:T(8,128)}) %all-reduce.5.cloned.1.call-update) | async-done | bytes 2949136 | tf_op jit(solution)/shard_map/psum | solution.py:133
  646.8 1.7 constant_dynamic-slice_fusion
  (68 shorter events, 9.0 us)
Async XLA Ops:
  7.2 50.9 %copy-start = (bf16[1,16,16,640]{3,2,1,0:T(8,128)(2,1)S(1)}, bf16[1,16,16,640]{3,2,1,0:T(8,128)(2,1)}, u32[]{:S(2)}) copy-start(bf16[1,16,16,640]{3,2,1,0:T(8,128)(2,1)} %param.8) | copy-start | bytes 983044
  7.2 314.9 %all-reduce.3.cloned.1.call-start = ((), (), s32[]{:S(2)}) async-start(), calls=%async_computation | async-start | bytes 655360 | tf_op jit(solution)/shard_map/psum | solution.py:131
  8.0 6.7 %collective-permute-start.1 = (bf16[1,16,640]{2,1,0:T(8,128)(2,1)S(1)}, bf16[1,16,640]{2,1,0:T(8,128)(2,1)S(1)}, u32[]{:S(2)}, u32[]{:S(2)}) collective-permute-start(bf16[1,16,640]{2,1,0:T(8,128)(2,1)S(1)} %get-tuple-element.33), channel_id=1, source_target_pairs={{4,0},{5,1},{6,2},{7,3},{12,8},{13,9},{14,10},{15,11},{20,16},{21,... | collective-permute-start | bytes 61448 | tf_op jit(solution)/shard_map/ppermute | solution.py:15
  9.3 5.4 collective-permute-start
  15.8 8.6 %collective-permute-start.3 = (bf16[18,1,640]{2,1,0:T(2,128)(2,1)S(1)}, bf16[18,1,640]{2,1,0:T(2,128)(2,1)S(1)}, u32[]{:S(2)}, u32[]{:S(2)}) collective-permute-start(bf16[18,1,640]{2,1,0:T(2,128)(2,1)S(1)} %get-tuple-element.24), channel_id=1, source_target_pairs={{0,1},{1,2},{2,3},{4,5},{5,6},{6,7},{8,9},{9,10},{10,11},{12,13},{... | collective-permute-start | bytes 69128 | tf_op jit(solution)/shard_map/ppermute | solution.py:14
  17.1 7.3 %collective-permute-start.2 = (bf16[18,1,640]{2,1,0:T(2,128)(2,1)S(1)}, bf16[18,1,640]{2,1,0:T(2,128)(2,1)S(1)}, u32[]{:S(2)}, u32[]{:S(2)}) collective-permute-start(bf16[18,1,640]{2,1,0:T(2,128)(2,1)S(1)} %get-tuple-element.25), channel_id=1, source_target_pairs={{1,0},{2,1},{3,2},{5,4},{6,5},{7,6},{9,8},{10,9},{11,10},{13,12},{... | collective-permute-start | bytes 69128 | tf_op jit(solution)/shard_map/ppermute | solution.py:15
  24.4 3.5 copy-start.3
  24.4 3.5 copy-start.6
  27.4 2.2 slice-start.4
  27.9 2.8 slice-start.5
  33.1 8.0 %copy-start.2 = (f32[9,640,640]{2,1,0:T(8,128)}, f32[9,640,640]{2,1,0:T(8,128)S(1)}, u32[]{:S(2)}) copy-start(f32[9,640,640]{2,1,0:T(8,128)S(1)} %bitcast_dynamic-update-slice_fusion.9) | copy-start | bytes 44236804
  33.5 7.5 %copy-start.5 = (f32[5760,2,64]{0,2,1:T(8,128)S(1)}, f32[5760,2,64]{0,2,1:T(8,128)}, u32[]{:S(2)}) copy-start(f32[5760,2,64]{0,2,1:T(8,128)} %param.12) | copy-start | bytes 8847364
  36.4 13.5 %collective-permute-start.5 = (bf16[1,16,640]{2,1,0:T(8,128)(2,1)S(1)}, bf16[1,16,640]{2,1,0:T(8,128)(2,1)S(1)}, u32[]{:S(2)}, u32[]{:S(2)}) collective-permute-start(bf16[1,16,640]{2,1,0:T(8,128)(2,1)S(1)} %get-tuple-element.29), channel_id=1, source_target_pairs={{4,0},{5,1},{6,2},{7,3},{12,8},{13,9},{14,10},{15,11},{20,16},{21,... | collective-permute-start | bytes 61448 | tf_op jit(solution)/shard_map/ppermute | solution.py:15
  37.8 12.1 %collective-permute-start.4 = (bf16[1,16,640]{2,1,0:T(8,128)(2,1)S(1)}, bf16[1,16,640]{2,1,0:T(8,128)(2,1)S(1)}, u32[]{:S(2)}, u32[]{:S(2)}) collective-permute-start(bf16[1,16,640]{2,1,0:T(8,128)(2,1)S(1)} %get-tuple-element.28), channel_id=1, source_target_pairs={{0,4},{1,5},{2,6},{3,7},{8,12},{9,13},{10,14},{11,15},{16,20},{17,... | collective-permute-start | bytes 61448 | tf_op jit(solution)/shard_map/ppermute | solution.py:14
  50.0 6.1 collective-permute-start.7
  51.3 6.3 collective-permute-start.6
  62.3 9.3 %copy-start.1 = (f32[9,640,640]{2,1,0:T(8,128)}, f32[9,640,640]{2,1,0:T(8,128)S(1)}, u32[]{:S(2)}) copy-start(f32[9,640,640]{2,1,0:T(8,128)S(1)} %bitcast_dynamic-update-slice_fusion) | copy-start | bytes 44236804
  72.3 574.5 %all-reduce.5.cloned.1.call-start = ((), (), s32[]{:S(2)}) async-start(), calls=%async_computation.1 | async-start | bytes 5898240 | tf_op jit(solution)/shard_map/psum | solution.py:133
  348.0 19.1 %slice-start = ((s8[14745600]{0:T(1024)(128)(4,1)}), s8[4194304]{0:T(1024)(128)(4,1)S(1)}, s32[]{:S(2)}) async-start(s8[14745600]{0:T(1024)(128)(4,1)} %bitcast.250), calls=%async_computation.2 | async-start | bytes 8388608
  349.4 17.3 %copy-start.4 = (f32[640,2,64]{0,2,1:T(8,128)S(1)}, f32[640,2,64]{0,2,1:T(8,128)}, u32[]{:S(2)}) copy-start(f32[640,2,64]{0,2,1:T(8,128)} %all-reduce.3.cloned.1.call-done) | copy-start | bytes 983044
  349.4 17.7 %slice-start.1 = ((s8[14745600]{0:T(1024)(128)(4,1)}), s8[4194304]{0:T(1024)(128)(4,1)S(1)}, s32[]{:S(2)}) async-start(s8[14745600]{0:T(1024)(128)(4,1)} %bitcast.250), calls=%async_computation.3 | async-start | bytes 8388608
  349.4 17.7 %slice-start.2 = ((s8[14745600]{0:T(1024)(128)(4,1)}), s8[4194304]{0:T(1024)(128)(4,1)S(1)}, s32[]{:S(2)}) async-start(s8[14745600]{0:T(1024)(128)(4,1)} %bitcast.250), calls=%async_computation.4 | async-start | bytes 8388608
  349.4 17.7 %slice-start.3 = ((s8[14745600]{0:T(1024)(128)(4,1)}), s8[2162688]{0:T(1024)(128)(4,1)S(1)}, s32[]{:S(2)}) async-start(s8[14745600]{0:T(1024)(128)(4,1)} %bitcast.250), calls=%async_computation.5 | async-start | bytes 4325376
Sparse Core Ops, SparseCore 0:
  72.4 249.5 all-reduce.2
  383.3 263.3 all-reduce.4
where the time goes:
time: 662 us; the launch traced here: 655 us
  waiting for transfers between devices  514 us (78%)
  matrix products  66.6 us (10%)
  other arithmetic  33.2 us (5%)
  starting transfers between devices  20.9 us (3%)
  between operations  14.8 us (2%)
    psum x1, waiting for transfers between devices, on_device(): lax.psum(row_terms(moments, ortho_basis), ('dp', 'row', 'col'))  263 us
    psum x1, waiting for transfers between devices, on_device(): power_raw = lax.psum(column_terms(moments, q_prev), ('dp', 'row', 'col'))  250 us
    dot_general x2, matrix products, row_terms(): jnp.dot(moments[layer], ortho_basis[:, layer, :], precision=lax.Precision...  31.5 us
    dot_general x2, matrix products, contract_first(): lax.dot_general(left, right, (((0,), (0,)), ((), ())), precision=lax.Prec...  18.1 us
  transfers between devices with their start and end apart: 10, of which 3 were waited for; matrix products, arithmetic and copies ran while one was open for 2% of the time, Pallas kernels for 0%

commit v1 on v0

--- a/solution.py
+++ b/solution.py
@@ -2,6 +2,7 @@
 import jax.numpy as jnp
 from jax import lax
 from jax.sharding import PartitionSpec as P
+from jax.lax import psum
 
 
 def padded_2(value, sides, width):
@@ -130,7 +131,9 @@
     factor_count = kernel_rows // lax.axis_size("dp")
     power_raw = lax.psum(column_terms(moments, q_prev), ("dp", "row", "col"))
     ortho_basis = orthonormal(power_raw, gram_of(power_raw))
-    factor_full = lax.psum(row_terms(moments, ortho_basis), ("dp", "row", "col"))
+    factor_full = psum(
+        psum(row_terms(moments, ortho_basis), axis_name="dp"), axis_name=("row", "col")
+    )
     basis_out = lax.dynamic_slice_in_dim(ortho_basis, owner * basis_count, basis_count, 0)
     factor_out = lax.dynamic_slice_in_dim(factor_full, owner * factor_count, factor_count, 0)
     return (basis_out, factor_out)

time: 662 us -> 627 us (0.947)
  waiting for transfers between devices: 514 us -> 477 us
    psum x1 -> x2, waiting for transfers between devices: 263 us -> 226 us  [the longest x1 156 us: on_device(): psum(row_terms(moments, ortho_basis), axis_name='dp')]
  transfers between devices with their start and end apart: 10 -> 11, of which waited for: 3 -> 4; matrix products, arithmetic and copies ran while one was open for 2% -> 2% of each run, Pallas kernels for 0% -> 0%
where the time goes in v1:
time: 627 us; the launch traced here: 618 us
  waiting for transfers between devices  477 us (76%)
  matrix products  66.6 us (11%)
  other arithmetic  33.2 us (5%)
  starting transfers between devices  20.9 us (3%)
  between operations  14.5 us (2%)
    psum x1, waiting for transfers between devices, on_device(): power_raw = lax.psum(column_terms(moments, q_prev), ('dp', 'row', 'col'))  250 us
    psum x1, waiting for transfers between devices, on_device(): psum(row_terms(moments, ortho_basis), axis_name='dp')  156 us
    psum x1, waiting for transfers between devices, on_device(): psum(psum(row_terms(moments, ortho_basis), axis_name='dp'), axis_name=('r...  69.8 us
    dot_general x2, matrix products, row_terms(): jnp.dot(moments[layer], ortho_basis[:, layer, :], precision=lax.Precision...  31.5 us
    dot_general x2, matrix products, contract_first(): lax.dot_general(left, right, (((0,), (0,)), ((), ())), precision=lax.Prec...  18.1 us
    another operation x6, other arithmetic, orthonormal(): lower = jnp.linalg.cholesky(gram_matrix[layer])  13.1 us
  transfers between devices with their start and end apart: 11, of which 4 were waited for; matrix products, arithmetic and copies ran while one was open for 2% of the time, Pallas kernels for 0%

profile of v1, /device:TPU:6, one launch (start us, length us, event | category | flops | bytes accessed | tf_op | source)
XLA Modules:
  0.0 618.1 jit_solution(10164900037713593646)
XLA Ops:
  7.2 0.8 slice_bitcast_fusion.9
  8.0 1.3 collective-permute-start.1
  9.3 3.0 collective-permute-start
  12.3 1.2 fusion.43
  13.5 1.2 fusion.38
  14.7 1.1 pad_maximum_fusion.11
  15.8 1.3 collective-permute-start.3
  17.1 4.5 collective-permute-start.2
  21.7 1.1 pad_maximum_fusion.5
  22.8 1.6 fusion.23
  24.5 1.4 maximum_maximum_fusion
  26.0 0.5 bitcast_dynamic-update-slice_fusion.17
  26.5 0.5 bitcast_dynamic-update-slice_fusion.16
  26.9 0.5 bitcast_dynamic-update-slice_fusion.15
  27.9 0.5 bitcast_dynamic-update-slice_fusion.13
  28.5 1.1 slice-done.4
  29.6 1.1 slice-done.5
  32.1 0.5 bitcast_dynamic-update-slice_fusion.10
  32.6 0.5 bitcast_dynamic-update-slice_fusion.9
  33.6 0.5 convolution_add_fusion.5
  34.5 0.5 convolution_add_fusion.3
  35.9 0.5 fusion.8
  36.4 1.4 collective-permute-start.5
  37.8 3.2 collective-permute-start.4
  41.1 8.8 %fusion.12 = f32[640,1,64]{0,2,1:T(8,128)S(1)} fusion(f32[5760,640]{1,0:T(8,128)S(1)} %bitcast.253, f32[5760,2,64]{0,2,1:T(8,128)S(1)} %copy-done.5), kind=kOutput, calls=%fused_computation.38 | convolution fusion | flops 2831155200 | bytes 16384000 | tf_op jit(solution)/shard_map/dot_general | solution.py:28
  50.0 1.3 collective-permute-start.7
  51.3 4.8 collective-permute-start.6
  56.1 1.4 collective-permute-done.6
  62.3 9.2 %fusion.9 = f32[640,1,64]{0,2,1:T(8,128)S(1)} fusion(f32[5760,640]{1,0:T(8,128)S(1)} %bitcast.249, f32[5760,2,64]{0,2,1:T(8,128)S(1)} %copy-done.5), kind=kOutput, calls=%fused_computation.37 | convolution fusion | flops 2831155200 | bytes 16384000 | tf_op jit(solution)/shard_map/dot_general | solution.py:28
  71.5 0.7 pad_maximum_fusion.7
  72.3 249.7 %all-reduce.4.cloned.1.call-done = f32[640,2,64]{0,2,1:T(8,128)} async-done(((f32[640,2,64]{0,2,1:T(8,128)}), f32[640,2,64]{0,2,1:T(8,128)}) %all-reduce.4.cloned.1.call-update) | async-done | bytes 327696 | tf_op jit(solution)/shard_map/psum | solution.py:132
  322.0 1.5 fusion.62
  323.8 5.8 cholesky.44
  329.7 0.6 compare_reduce_fusion.1
  330.3 0.7 fusion.50
  331.0 4.9 custom-call.6
  335.9 5.9 cholesky.55
  341.8 0.6 compare_reduce_fusion
  342.4 0.7 fusion.51
  343.1 4.9 custom-call.7
  348.0 1.4 fusion.45
  349.4 17.3 %convolution_bitcast_fusion = f32[5760,1,64]{0,2,1:T(8,128)S(1)} fusion(f32[5760,640]{1,0:T(8,128)} %bitcast.254, f32[64,640]{1,0:T(8,128)S(1)} %fusion.45), kind=kOutput, calls=%fused_computation | convolution fusion | flops 2831155200 | bytes 16384000 | tf_op jit(solution)/shard_map/dot_general | solution.py:55
  367.1 14.2 %convolution_bitcast_fusion.1 = f32[5760,1,64]{0,2,1:T(8,128)S(1)} fusion(f32[5760,640]{1,0:T(8,128)S(1)} %bitcast.252, f32[64,640]{1,0:T(8,128)S(1)} %fusion.46), kind=kOutput, calls=%fused_computation.1 | convolution fusion | flops 2831155200 | bytes 16384000 | tf_op jit(solution)/shard_map/dot_general | solution.py:55
  381.4 1.8 pad_maximum_fusion
  383.2 155.9 %all-reduce.6.cloned.1.call-done = f32[5760,2,64]{0,2,1:T(8,128)} async-done(((f32[5760,2,64]{0,2,1:T(8,128)}), f32[5760,2,64]{0,2,1:T(8,128)}) %all-reduce.6.cloned.1.call-update) | async-done | bytes 2949136 | tf_op jit(solution)/shard_map/psum | solution.py:135
  539.2 0.7 copy.11
  539.9 69.8 %all-reduce.8.cloned.1.call-done = f32[5760,2,64]{0,2,1:T(8,128)} async-done(((f32[5760,2,64]{0,2,1:T(8,128)}), f32[5760,2,64]{0,2,1:T(8,128)}) %all-reduce.8.cloned.1.call-update) | async-done | bytes 2949136 | tf_op jit(solution)/shard_map/psum | solution.py:134
  609.7 1.7 constant_dynamic-slice_fusion
  (71 shorter events, 9.6 us)
Async XLA Ops:
  7.2 50.9 %copy-start = (bf16[1,16,16,640]{3,2,1,0:T(8,128)(2,1)S(1)}, bf16[1,16,16,640]{3,2,1,0:T(8,128)(2,1)}, u32[]{:S(2)}) copy-start(bf16[1,16,16,640]{3,2,1,0:T(8,128)(2,1)} %param.8) | copy-start | bytes 983044
  7.2 314.9 %all-reduce.4.cloned.1.call-start = ((), (), s32[]{:S(2)}) async-start(), calls=%async_computation | async-start | bytes 655360 | tf_op jit(solution)/shard_map/psum | solution.py:132
  8.0 6.7 %collective-permute-start.1 = (bf16[1,16,640]{2,1,0:T(8,128)(2,1)S(1)}, bf16[1,16,640]{2,1,0:T(8,128)(2,1)S(1)}, u32[]{:S(2)}, u32[]{:S(2)}) collective-permute-start(bf16[1,16,640]{2,1,0:T(8,128)(2,1)S(1)} %get-tuple-element.33), channel_id=1, source_target_pairs={{4,0},{5,1},{6,2},{7,3},{12,8},{13,9},{14,10},{15,11},{20,16},{21,... | collective-permute-start | bytes 61448 | tf_op jit(solution)/shard_map/ppermute | solution.py:16
  9.3 5.4 collective-permute-start
  15.8 8.6 %collective-permute-start.3 = (bf16[18,1,640]{2,1,0:T(2,128)(2,1)S(1)}, bf16[18,1,640]{2,1,0:T(2,128)(2,1)S(1)}, u32[]{:S(2)}, u32[]{:S(2)}) collective-permute-start(bf16[18,1,640]{2,1,0:T(2,128)(2,1)S(1)} %get-tuple-element.24), channel_id=1, source_target_pairs={{0,1},{1,2},{2,3},{4,5},{5,6},{6,7},{8,9},{9,10},{10,11},{12,13},{... | collective-permute-start | bytes 69128 | tf_op jit(solution)/shard_map/ppermute | solution.py:15
  17.1 7.3 %collective-permute-start.2 = (bf16[18,1,640]{2,1,0:T(2,128)(2,1)S(1)}, bf16[18,1,640]{2,1,0:T(2,128)(2,1)S(1)}, u32[]{:S(2)}, u32[]{:S(2)}) collective-permute-start(bf16[18,1,640]{2,1,0:T(2,128)(2,1)S(1)} %get-tuple-element.25), channel_id=1, source_target_pairs={{1,0},{2,1},{3,2},{5,4},{6,5},{7,6},{9,8},{10,9},{11,10},{13,12},{... | collective-permute-start | bytes 69128 | tf_op jit(solution)/shard_map/ppermute | solution.py:16
  24.4 3.5 copy-start.3
  24.4 3.5 copy-start.6
  27.4 2.2 slice-start.4
  27.9 2.8 slice-start.5
  33.1 8.0 %copy-start.2 = (f32[9,640,640]{2,1,0:T(8,128)}, f32[9,640,640]{2,1,0:T(8,128)S(1)}, u32[]{:S(2)}) copy-start(f32[9,640,640]{2,1,0:T(8,128)S(1)} %bitcast_dynamic-update-slice_fusion.9) | copy-start | bytes 44236804
  33.5 7.5 %copy-start.5 = (f32[5760,2,64]{0,2,1:T(8,128)S(1)}, f32[5760,2,64]{0,2,1:T(8,128)}, u32[]{:S(2)}) copy-start(f32[5760,2,64]{0,2,1:T(8,128)} %param.12) | copy-start | bytes 8847364
  36.4 13.5 %collective-permute-start.5 = (bf16[1,16,640]{2,1,0:T(8,128)(2,1)S(1)}, bf16[1,16,640]{2,1,0:T(8,128)(2,1)S(1)}, u32[]{:S(2)}, u32[]{:S(2)}) collective-permute-start(bf16[1,16,640]{2,1,0:T(8,128)(2,1)S(1)} %get-tuple-element.29), channel_id=1, source_target_pairs={{4,0},{5,1},{6,2},{7,3},{12,8},{13,9},{14,10},{15,11},{20,16},{21,... | collective-permute-start | bytes 61448 | tf_op jit(solution)/shard_map/ppermute | solution.py:16
  37.8 12.1 %collective-permute-start.4 = (bf16[1,16,640]{2,1,0:T(8,128)(2,1)S(1)}, bf16[1,16,640]{2,1,0:T(8,128)(2,1)S(1)}, u32[]{:S(2)}, u32[]{:S(2)}) collective-permute-start(bf16[1,16,640]{2,1,0:T(8,128)(2,1)S(1)} %get-tuple-element.28), channel_id=1, source_target_pairs={{0,4},{1,5},{2,6},{3,7},{8,12},{9,13},{10,14},{11,15},{16,20},{17,... | collective-permute-start | bytes 61448 | tf_op jit(solution)/shard_map/ppermute | solution.py:15
  50.0 6.1 collective-permute-start.7
  51.3 6.3 %collective-permute-start.6 = (bf16[18,1,640]{2,1,0:T(2,128)(2,1)S(1)}, bf16[18,1,640]{2,1,0:T(2,128)(2,1)S(1)}, u32[]{:S(2)}, u32[]{:S(2)}) collective-permute-start(bf16[18,1,640]{2,1,0:T(2,128)(2,1)S(1)} %get-tuple-element.21), channel_id=1, source_target_pairs={{1,0},{2,1},{3,2},{5,4},{6,5},{7,6},{9,8},{10,9},{11,10},{13,12},{... | collective-permute-start | bytes 69128 | tf_op jit(solution)/shard_map/ppermute | solution.py:16
  62.3 9.3 %copy-start.1 = (f32[9,640,640]{2,1,0:T(8,128)}, f32[9,640,640]{2,1,0:T(8,128)S(1)}, u32[]{:S(2)}) copy-start(f32[9,640,640]{2,1,0:T(8,128)S(1)} %bitcast_dynamic-update-slice_fusion) | copy-start | bytes 44236804
  72.3 466.8 %all-reduce.6.cloned.1.call-start = ((), (), s32[]{:S(2)}) async-start(), calls=%async_computation.1 | async-start | bytes 5898240 | tf_op jit(solution)/shard_map/psum | solution.py:135
  348.0 19.1 %slice-start = ((s8[14745600]{0:T(1024)(128)(4,1)}), s8[4194304]{0:T(1024)(128)(4,1)S(1)}, s32[]{:S(2)}) async-start(s8[14745600]{0:T(1024)(128)(4,1)} %bitcast.250), calls=%async_computation.3 | async-start | bytes 8388608
  349.4 17.3 %copy-start.4 = (f32[640,2,64]{0,2,1:T(8,128)S(1)}, f32[640,2,64]{0,2,1:T(8,128)}, u32[]{:S(2)}) copy-start(f32[640,2,64]{0,2,1:T(8,128)} %all-reduce.4.cloned.1.call-done) | copy-start | bytes 983044
  349.4 17.7 %slice-start.1 = ((s8[14745600]{0:T(1024)(128)(4,1)}), s8[4194304]{0:T(1024)(128)(4,1)S(1)}, s32[]{:S(2)}) async-start(s8[14745600]{0:T(1024)(128)(4,1)} %bitcast.250), calls=%async_computation.4 | async-start | bytes 8388608
  349.4 17.7 %slice-start.2 = ((s8[14745600]{0:T(1024)(128)(4,1)}), s8[4194304]{0:T(1024)(128)(4,1)S(1)}, s32[]{:S(2)}) async-start(s8[14745600]{0:T(1024)(128)(4,1)} %bitcast.250), calls=%async_computation.5 | async-start | bytes 8388608
  349.4 17.7 %slice-start.3 = ((s8[14745600]{0:T(1024)(128)(4,1)}), s8[2162688]{0:T(1024)(128)(4,1)S(1)}, s32[]{:S(2)}) async-start(s8[14745600]{0:T(1024)(128)(4,1)} %bitcast.250), calls=%async_computation.6 | async-start | bytes 4325376
  383.2 226.5 %all-reduce.8.cloned.1.call-start = ((), (), s32[]{:S(2)}) async-start(), calls=%async_computation.2 | async-start | bytes 5898240 | tf_op jit(solution)/shard_map/psum | solution.py:134
Sparse Core Ops, SparseCore 0:
  72.4 249.5 all-reduce.3
  383.3 155.7 all-reduce.5
  541.6 68.0 all-reduce.7
